TPU v7x, 32 devices: a whole 2x2x4 slice. The times are simulated.
32 devices in a mesh: row: 2 (over y), col: 16 (over z, x, core).
Axes of the slice: x: 2, y: 2, z: 4, core: 2. Of those that a mesh axis runs over, the one named last changes fastest.
Arguments:
- blocks: bfloat16 [128, 2048, 128], P('row', 'col'), may hold values from -0.1875 to 0.1875
- block_rows: int32 [2, 1024], P('row', 'col'), may hold values from 0 to 2047, as said below
- block_cols: int32 [2, 1024], P('row', 'col'), may hold values from 0 to 255
- counts: int32 [2, 16], P('row', 'col'), may hold values from 1 to 64, as said below
- start_vectors: float32 [32, 524288], P(None, ('row', 'col')), may hold values from -6 to 6
Outputs:
- vectors: float32 [32, 524288], P(None, ('row', 'col'))
Inputs may be any that keep to these rules, and one draw needn't show every extreme that they name: counts[r, c] is the number of live slots of grid position (r, c); in every draw some position has all 64 slots live. For every grid position (r, c) and every o < 16, exactly 4 of its 64 slots have block_rows[r, c * 64 + s] // 128 == o.
All inputs are finite; a program needn't handle non-finite values.
Results may differ from a plain program's by a relative error of at most 0.0036.
Values may be sent and summed in bfloat16 or wider, within the bound.
A program may use at most 256 MiB of HBM per device.

v0:
```python
import math
import jax
import jax.numpy as jnp
from jax import lax
from jax.sharding import PartitionSpec as P

N = 524288
ITERS = 2


def cholesky_lower(gram_matrix):
    matrix_order = gram_matrix.shape[0]
    positions = jnp.arange(matrix_order)

    def column_step(position, factor):
        before = (positions < position).astype(gram_matrix.dtype)
        target_row = lax.dynamic_index_in_dim(factor, position, 0, keepdims=False) * before
        column = lax.dynamic_index_in_dim(gram_matrix, position, 1, keepdims=False)
        residue = column - jnp.sum(factor * target_row[None, :], axis=1)
        on_diagonal = positions == position
        pivot_value = jnp.sqrt(jnp.sum(jnp.where(on_diagonal, residue, 0.0)))
        values = jnp.where(on_diagonal, pivot_value, residue / pivot_value)
        values = jnp.where(positions >= position, values, 0.0)
        return lax.dynamic_update_index_in_dim(factor, values, position, 1)

    return lax.fori_loop(0, matrix_order, column_step, jnp.zeros_like(gram_matrix))


def lower_inverse(lower_factor):
    matrix_order = lower_factor.shape[0]
    positions = jnp.arange(matrix_order)

    def row_step(position, inverse):
        lower_row = lax.dynamic_index_in_dim(lower_factor, position, 0, keepdims=False)
        before = (positions < position).astype(lower_factor.dtype)
        inner_sum = jnp.sum((lower_row * before)[:, None] * inverse, axis=0)
        unit_row = (positions == position).astype(lower_factor.dtype)
        pivot_value = jnp.sum(lower_row * unit_row)
        return lax.dynamic_update_index_in_dim(
            inverse, (unit_row - inner_sum) / pivot_value, position, 0
        )

    return lax.fori_loop(0, matrix_order, row_step, jnp.zeros_like(lower_factor))


def accumulate(blocks, rows_index, cols_index, live_count, row_panel, col_panel):
    slot_count, block_size = (blocks.shape[0], blocks.shape[1])
    vector_count = row_panel.shape[0]
    row_blocks = row_panel.reshape(vector_count, -1, block_size)
    col_blocks = col_panel.reshape(vector_count, -1, block_size)
    group_size = math.gcd(slot_count, 64)
    turn_count = (live_count + group_size - 1) // group_size
    slot_offsets = jnp.arange(group_size, dtype=jnp.int32)

    def one_group(turn_index, partial_sums):
        row_sums, col_sums = partial_sums
        first_slot = turn_index * group_size
        live_mask = (first_slot + slot_offsets < live_count).astype(jnp.float32)
        from_cols = jnp.take(col_blocks, cols_index, axis=1)
        from_rows = jnp.take(row_blocks, rows_index, axis=1)
        to_cols = jnp.einsum("kgi,gij->kgj", from_rows, blocks, preferred_element_type=jnp.float32)
        col_sums = col_sums.at[:, cols_index].add(to_cols * live_mask[None, :, None])
        to_rows = jnp.einsum("kgj,gij->kgi", from_cols, blocks, preferred_element_type=jnp.float32)
        row_sums = row_sums.at[:, rows_index].add(to_rows * live_mask[None, :, None])
        return (row_sums, col_sums)

    row_start = jnp.zeros(row_blocks.shape, jnp.float32)
    initial = (row_start, jnp.zeros(col_blocks.shape, jnp.float32))
    return lax.fori_loop(0, turn_count, one_group, initial)


def per_device(blocks, block_rows, block_cols, counts, start_vectors):
    live_count = counts[0, 0]
    rows_index = block_rows[0]
    cols_index = block_cols[0]
    vectors = start_vectors
    for iteration in range(ITERS):
        rounded = vectors.astype(jnp.bfloat16)
        vector_count = rounded.shape[0]
        col_panel = lax.all_gather(rounded, "row", axis=1, tiled=True)
        row_panel = lax.all_gather(rounded, "col", axis=1, tiled=True)
        row_sums, col_sums = accumulate(
            blocks, rows_index, cols_index, live_count, row_panel, col_panel
        )
        from_row_group = lax.psum_scatter(
            row_sums.reshape(vector_count, -1), "col", scatter_dimension=1, tiled=True
        )
        from_col_group = lax.psum_scatter(
            col_sums.reshape(vector_count, -1), "row", scatter_dimension=1, tiled=True
        )
        product = from_row_group + from_col_group
        local_gram = jnp.dot(
            product, product.T, precision=lax.Precision.HIGHEST, preferred_element_type=jnp.float32
        )
        gram_matrix = lax.psum(local_gram, ("row", "col")) / N
        inverse = lower_inverse(cholesky_lower(gram_matrix))
        vectors = jnp.dot(
            inverse, product, precision=lax.Precision.HIGHEST, preferred_element_type=jnp.float32
        )
    return vectors


def solution(mesh):
    placed = (
        P("row", "col", None),
        P("row", "col"),
        P("row", "col"),
        P("row", "col"),
        P(None, ("row", "col")),
    )
    return jax.shard_map(
        per_device, mesh=mesh, in_specs=placed, out_specs=P(None, ("row", "col")), check_vma=False
    )
```

profile of v0, /device:TPU:0, one launch (start us, length us, event | category | flops | bytes accessed | tf_op | source)
XLA Modules:
  0.0 1549.7 jit_solution(5209276909103308987)
XLA Ops:
  6.5 2.8 convert_element_type.66
  11.0 34.4 %all-gather.5.cloned.1.call-done = bf16[32,32768]{1,0:T(8,128)(2,1)} async-done(((bf16[32,16384]{1,0:T(8,128)(2,1)}), bf16[32,32768]{1,0:T(8,128)(2,1)}) %all-gather.5.cloned.1.call-update) | async-done | bytes 2097168 | tf_op jit(solution)/shard_map/all_gather | solution.py:80
  45.4 3.3 copy_bitcast_fusion.7
  48.6 2.2 gather_fusion
  50.9 2.2 fusion.34
  53.1 121.4 %all-gather.7.cloned.1.call-done = bf16[32,262144]{1,0:T(8,128)(2,1)} async-done(((bf16[32,16384]{1,0:T(8,128)(2,1)}), bf16[32,262144]{1,0:T(8,128)(2,1)}) %all-gather.7.cloned.1.call-update) | async-done | bytes 16777232 | tf_op jit(solution)/shard_map/all_gather | solution.py:81
  174.5 14.5 copy_bitcast_fusion.3
  189.0 6.4 gather_fusion.1
  195.4 1.7 fusion.32
  197.1 11.3 broadcast.314.clone
  208.4 2.6 broadcast.315.clone
  210.9 20.4 %while.90 = (s32[]{:T(128)}, f32[32,2048,128]{2,0,1:T(8,128)}, f32[32,256,128]{2,0,1:T(8,128)}, s32[]{:T(128)}, s32[64]{0:T(128)S(1)}, /*index=5*/s32[]{:T(128)}...) while((s32[]{:T(128)}, f32[32,2048,128]{2,0,1:T(8,128)}, ...), condition=%wide.region_3.6_spmd.clone, body=%wide.region_0.5_spmd.clone.sunk | while | flops 1049155 | bytes 10487937 | solution.py:69
  211.6 2.7 broadcast_multiply_fusion.8
  214.3 9.0 scatter_fusion
  223.3 8.0 scatter_fusion.1
  231.3 4.4 copy_bitcast_fusion.5
  235.8 22.6 %copy_bitcast_fusion.1 = f32[32,262144]{1,0:T(8,128)} fusion(f32[32,2048,128]{2,0,1:T(8,128)} %get-tuple-element.609), kind=kLoop, calls=%fused_computation.69 | loop fusion | bytes 67108864 | tf_op jit(solution)/shard_map/reshape | solution.py:86
  258.5 30.0 %reduce-scatter.7.cloned.1.call-done = f32[32,16384]{1,0:T(8,128)} async-done(((f32[32,32768]{1,0:T(8,128)}), f32[32,16384]{1,0:T(8,128)}) %reduce-scatter.7.cloned.1.call-update) | async-done | bytes 2097168 | tf_op jit(solution)/shard_map/reduce_scatter | solution.py:88
  288.4 337.4 %reduce-scatter.5.cloned.1.call-done = f32[32,16384]{1,0:T(8,128)} async-done(((f32[32,262144]{1,0:T(8,128)}), f32[32,16384]{1,0:T(8,128)}) %reduce-scatter.5.cloned.1.call-update) | async-done | bytes 2097168 | tf_op jit(solution)/shard_map/reduce_scatter | solution.py:85
  625.8 2.4 add.220
  629.5 1.8 fusion.52
  631.3 39.1 %psum.14 = f32[32,32]{1,0:T(8,128)S(1)} all-reduce(f32[32,32]{1,0:T(8,128)S(1)} %fusion.52), channel_id=1, replica_groups=mesh['row'=2,'col'=16] {'row','col'}, use_global_device_ids=true, to_apply=%region_6.9 | all-reduce | flops 1024 | bytes 8192 | tf_op jit(solution)/shard_map/psum | solution.py:95
  670.4 58.1 %while.92 = (s32[]{:T(128)}, f32[32,32]{1,0:T(8,128)S(1)}, f32[32,32]{0,1:T(8,128)S(1)}, s32[]{:T(128)}, s32[]{:T(128)}) while((s32[]{:T(128)}, f32[32,32]{1,0:T(8,128)S(1)}, f32[32,32]{0,1:T(8,128)S(1)}, s32[]{:T(128)}, s32[]{:T(128)}) %tuple.192), condition=%wide.region_10.13_spmd.clone.clone, body=%wide.region_7.12_spmd.clone.clone.sunk | while | flops 2401 | bytes 8913 | solution.py:26
  728.6 49.0 %while.93 = (s32[]{:T(128)}, f32[32,32]{1,0:T(8,128)S(1)}, f32[32,32]{1,0:T(8,128)S(1)}, s32[]{:T(128)}, s32[]{:T(128)}) while((s32[]{:T(128)}, f32[32,32]{1,0:T(8,128)S(1)}, f32[32,32]{1,0:T(8,128)S(1)}, s32[]{:T(128)}, s32[]{:T(128)}) %tuple.195), condition=%wide.region_14.17_spmd.clone.clone, body=%wide.region_11.16_spmd.clone.clone.sunk | while | flops 2305 | bytes 6221 | solution.py:43
  777.6 4.4 convolution_convert_fusion
  782.8 32.2 %all-gather.9.cloned.1.call-done = bf16[32,32768]{1,0:T(8,128)(2,1)} async-done(((bf16[32,16384]{1,0:T(8,128)(2,1)}), bf16[32,32768]{1,0:T(8,128)(2,1)}) %all-gather.9.cloned.1.call-update) | async-done | bytes 2097168 | tf_op jit(solution)/shard_map/all_gather | solution.py:80
  815.1 3.3 copy_bitcast_fusion.6
  818.3 2.2 gather_fusion.2
  820.6 2.2 fusion.30
  822.8 121.5 %all-gather.11.cloned.1.call-done = bf16[32,262144]{1,0:T(8,128)(2,1)} async-done(((bf16[32,16384]{1,0:T(8,128)(2,1)}), bf16[32,262144]{1,0:T(8,128)(2,1)}) %all-gather.11.cloned.1.call-update) | async-done | bytes 16777232 | tf_op jit(solution)/shard_map/all_gather | solution.py:81
  944.3 14.5 copy_bitcast_fusion.2
  958.8 6.4 gather_fusion.3
  966.9 11.3 broadcast.314
  978.2 2.6 broadcast.315
  980.7 20.4 %while.91 = (s32[]{:T(128)}, f32[32,2048,128]{2,0,1:T(8,128)}, f32[32,256,128]{2,0,1:T(8,128)}, s32[]{:T(128)}, s32[64]{0:T(128)S(1)}, /*index=5*/s32[]{:T(128)}...) while((s32[]{:T(128)}, f32[32,2048,128]{2,0,1:T(8,128)}, ...), condition=%wide.region_18.21_spmd.clone, body=%wide.region_15.20_spmd.clone.sunk | while | flops 1049155 | bytes 10487937 | solution.py:69
  981.4 2.7 broadcast_multiply_fusion.9
  984.1 9.0 scatter_fusion.2
  993.1 8.0 scatter_fusion.3
  1001.1 4.4 copy_bitcast_fusion.4
  1005.6 22.6 %copy_bitcast_fusion = f32[32,262144]{1,0:T(8,128)} fusion(f32[32,2048,128]{2,0,1:T(8,128)} %get-tuple-element.613), kind=kLoop, calls=%fused_computation.68 | loop fusion | bytes 67108864 | tf_op jit(solution)/shard_map/reshape | solution.py:86
  1028.2 30.0 %reduce-scatter.11.cloned.1.call-done = f32[32,16384]{1,0:T(8,128)} async-done(((f32[32,32768]{1,0:T(8,128)}), f32[32,16384]{1,0:T(8,128)}) %reduce-scatter.11.cloned.1.call-update) | async-done | bytes 2097168 | tf_op jit(solution)/shard_map/reduce_scatter | solution.py:88
  1058.2 336.9 %reduce-scatter.9.cloned.1.call-done = f32[32,16384]{1,0:T(8,128)} async-done(((f32[32,262144]{1,0:T(8,128)}), f32[32,16384]{1,0:T(8,128)}) %reduce-scatter.9.cloned.1.call-update) | async-done | bytes 2097168 | tf_op jit(solution)/shard_map/reduce_scatter | solution.py:85
  1395.2 2.4 add.221
  1398.9 1.8 fusion.53
  1400.7 39.0 %psum.15 = f32[32,32]{1,0:T(8,128)S(1)} all-reduce(f32[32,32]{1,0:T(8,128)S(1)} %fusion.53), channel_id=1, replica_groups=mesh['row'=2,'col'=16] {'row','col'}, use_global_device_ids=true, to_apply=%region_21.24 | all-reduce | flops 1024 | bytes 8192 | tf_op jit(solution)/shard_map/psum | solution.py:95
  1439.8 53.9 %while.94 = (s32[]{:T(128)}, f32[32,32]{1,0:T(8,128)S(1)}, f32[32,32]{0,1:T(8,128)S(1)}, s32[]{:T(128)}, s32[]{:T(128)}) while((s32[]{:T(128)}, f32[32,32]{1,0:T(8,128)S(1)}, f32[32,32]{0,1:T(8,128)S(1)}, s32[]{:T(128)}, s32[]{:T(128)}) %tuple.201), condition=%wide.region_25.28_spmd.clone.clone, body=%wide.region_22.27_spmd.clone.clone.sunk | while | flops 2401 | bytes 8913 | solution.py:26
  1493.7 44.3 %while.95 = (s32[]{:T(128)}, f32[32,32]{1,0:T(8,128)S(1)}, f32[32,32]{1,0:T(8,128)S(1)}, s32[]{:T(128)}, s32[]{:T(128)}) while((s32[]{:T(128)}, f32[32,32]{1,0:T(8,128)S(1)}, f32[32,32]{1,0:T(8,128)S(1)}, s32[]{:T(128)}, s32[]{:T(128)}) %tuple.204), condition=%wide.region_29.32_spmd.clone.clone, body=%wide.region_26.31_spmd.clone.clone.sunk | while | flops 2305 | bytes 6221 | solution.py:43
  1538.1 4.8 fusion.54
  (685 shorter events, 164.6 us)
Async XLA Ops:
  6.5 44.4 %copy-start = (bf16[64,128,128]{2,1,0:T(8,128)(2,1)S(1)}, bf16[64,128,128]{2,1,0:T(8,128)(2,1)}, u32[]{:S(2)}) copy-start(bf16[64,128,128]{2,1,0:T(8,128)(2,1)} %param.21) | copy-start | bytes 6291460
  6.5 4.3 copy-start.3
  6.5 4.4 copy-start.4
  6.5 38.8 %all-gather.5.cloned.1.call-start = ((), (), s32[]{:S(2)}) async-start(), calls=%async_computation.4 | async-start | bytes 3145728 | tf_op jit(solution)/shard_map/all_gather | solution.py:80
  9.4 165.1 %all-gather.7.cloned.1.call-start = ((), (), s32[]{:S(2)}) async-start(), calls=%async_computation.5 | async-start | bytes 17825792 | tf_op jit(solution)/shard_map/all_gather | solution.py:81
  10.2 278.3 %reduce-scatter.7.cloned.1.call-start = ((), (), s32[]{:S(2)}) async-start(), calls=%async_computation.7 | async-start | bytes 6291456 | tf_op jit(solution)/shard_map/reduce_scatter | solution.py:88
  235.8 390.0 %reduce-scatter.5.cloned.1.call-start = ((), (), s32[]{:S(2)}) async-start(), calls=%async_computation.6 | async-start | bytes 35651584 | tf_op jit(solution)/shard_map/reduce_scatter | solution.py:85
  258.4 556.7 %all-gather.9.cloned.1.call-start = ((), (), s32[]{:S(2)}) async-start(), calls=%async_computation.8 | async-start | bytes 3145728 | tf_op jit(solution)/shard_map/all_gather | solution.py:80
  628.2 1.3 copy-start.2
  782.0 162.3 %all-gather.11.cloned.1.call-start = ((), (), s32[]{:S(2)}) async-start(), calls=%async_computation.9 | async-start | bytes 17825792 | tf_op jit(solution)/shard_map/all_gather | solution.py:81
  782.6 275.6 %reduce-scatter.11.cloned.1.call-start = ((), (), s32[]{:S(2)}) async-start(), calls=%async_computation.11 | async-start | bytes 6291456 | tf_op jit(solution)/shard_map/reduce_scatter | solution.py:88
  1005.6 389.6 %reduce-scatter.9.cloned.1.call-start = ((), (), s32[]{:S(2)}) async-start(), calls=%async_computation.10 | async-start | bytes 35651584 | tf_op jit(solution)/shard_map/reduce_scatter | solution.py:85
  1397.6 1.4 copy-start.1
Sparse Core Ops, SparseCore 0:
  9.5 35.8 all-gather.4
  47.6 126.9 all-gather.6
  235.9 52.4 reduce-scatter.6
  293.1 332.6 reduce-scatter.4
  782.1 32.8 all-gather.8
  817.4 126.9 all-gather.10
  1005.7 52.4 reduce-scatter.10
  1062.5 332.6 reduce-scatter.8
where the time goes:
time: 1550 us
  waiting for transfers between devices  1050 us (68%)
  other arithmetic  189 us (12%)
  local copies, waits for them, and re-layouts  153 us (10%)
  blocking collectives  78.1 us (5%)
  loops' own time  48.3 us (3%)
  matrix products  20.5 us (1%)
    reduce_scatter x2, waiting for transfers between devices, per_device(): lax.psum_scatter(row_sums.reshape(vector_count, -1), 'col', scatter_dimen...  674 us
    all_gather x2, waiting for transfers between devices, per_device(): row_panel = lax.all_gather(rounded, 'col', axis=1, tiled=True)  243 us
    psum x2, blocking collectives, per_device(): gram_matrix = lax.psum(local_gram, ('row', 'col')) / N  78.1 us
    all_gather x2, waiting for transfers between devices, per_device(): col_panel = lax.all_gather(rounded, 'row', axis=1, tiled=True)  66.7 us
    reduce_scatter x2, waiting for transfers between devices, per_device(): lax.psum_scatter(col_sums.reshape(vector_count, -1), 'row', scatter_dimen...  60 us
    another operation x2, loops' own time, cholesky_lower(): lax.fori_loop(0, matrix_order, column_step, jnp.zeros_like(gram_matrix))  46.9 us
    reshape x2, local copies, waits for them, and re-layouts, per_device(): row_sums.reshape(vector_count, -1)  45.2 us
    reduce_sum x64, other arithmetic, column_step(): pivot_value = jnp.sqrt(jnp.sum(jnp.where(on_diagonal, residue, 0.0)))  42.8 us
  transfers between devices with their start and end apart: 8, of which 8 were waited for; matrix products, arithmetic and copies ran while one was open for 4% of the time, Pallas kernels for 0%

commit v1 on v0

--- a/solution.py
+++ b/solution.py
@@ -92,7 +92,7 @@
         local_gram = jnp.dot(
             product, product.T, precision=lax.Precision.HIGHEST, preferred_element_type=jnp.float32
         )
-        gram_matrix = lax.psum(local_gram, ("row", "col")) / N
+        gram_matrix = jnp.sum(lax.all_gather(local_gram, ("row", "col")), axis=0) / N
         inverse = lower_inverse(cholesky_lower(gram_matrix))
         vectors = jnp.dot(
             inverse, product, precision=lax.Precision.HIGHEST, preferred_element_type=jnp.float32

time: 1550 us -> 1550 us (level)
    all_gather x0 -> x2, blocking collectives: none -> 82 us  [per_device(): lax.all_gather(local_gram, ('row', 'col'))]
    psum x2 -> x0, blocking collectives: 78.1 us -> none  [per_device(): gram_matrix = lax.psum(local_gram, ('row', 'col')) / N]
where the time goes in v1:
time: 1550 us
  waiting for transfers between devices  1040 us (67%)
  other arithmetic  190 us (12%)
  local copies, waits for them, and re-layouts  153 us (10%)
  blocking collectives  82 us (5%)
  loops' own time  48.3 us (3%)
  matrix products  20.5 us (1%)
    reduce_scatter x2, waiting for transfers between devices, per_device(): lax.psum_scatter(row_sums.reshape(vector_count, -1), 'col', scatter_dimen...  674 us
    all_gather x2, waiting for transfers between devices, per_device(): row_panel = lax.all_gather(rounded, 'col', axis=1, tiled=True)  243 us
    all_gather x2, blocking collectives, per_device(): lax.all_gather(local_gram, ('row', 'col'))  82 us
    all_gather x2, waiting for transfers between devices, per_device(): col_panel = lax.all_gather(rounded, 'row', axis=1, tiled=True)  63.2 us
    reduce_scatter x2, waiting for transfers between devices, per_device(): lax.psum_scatter(col_sums.reshape(vector_count, -1), 'row', scatter_dimen...  60 us
    another operation x2, loops' own time, cholesky_lower(): lax.fori_loop(0, matrix_order, column_step, jnp.zeros_like(gram_matrix))  46.9 us
    reshape x2, local copies, waits for them, and re-layouts, per_device(): row_sums.reshape(vector_count, -1)  45.2 us
    reduce_sum x64, other arithmetic, column_step(): pivot_value = jnp.sqrt(jnp.sum(jnp.where(on_diagonal, residue, 0.0)))  42.8 us
  transfers between devices with their start and end apart: 8, of which 8 were waited for; matrix products, arithmetic and copies ran while one was open for 4% of the time, Pallas kernels for 0%

profile of v1, /device:TPU:0, one launch (start us, length us, event | category | flops | bytes accessed | tf_op | source)
XLA Modules:
  0.0 1550.3 jit_solution(10772618701418687809)
XLA Ops:
  6.5 2.8 convert_element_type.66
  11.0 34.4 %all-gather.7.cloned.1.call-done = bf16[32,32768]{1,0:T(8,128)(2,1)} async-done(((bf16[32,16384]{1,0:T(8,128)(2,1)}), bf16[32,32768]{1,0:T(8,128)(2,1)}) %all-gather.7.cloned.1.call-update) | async-done | bytes 2097168 | tf_op jit(solution)/shard_map/all_gather | solution.py:80
  45.4 3.3 copy_bitcast_fusion.7
  48.6 2.2 gather_fusion
  50.9 2.2 fusion.34
  53.1 121.4 %all-gather.9.cloned.1.call-done = bf16[32,262144]{1,0:T(8,128)(2,1)} async-done(((bf16[32,16384]{1,0:T(8,128)(2,1)}), bf16[32,262144]{1,0:T(8,128)(2,1)}) %all-gather.9.cloned.1.call-update) | async-done | bytes 16777232 | tf_op jit(solution)/shard_map/all_gather | solution.py:81
  174.5 14.5 copy_bitcast_fusion.3
  189.0 6.4 gather_fusion.1
  195.4 1.7 fusion.32
  197.1 11.3 broadcast.314.clone
  208.4 2.6 broadcast.315.clone
  210.9 20.4 %while.90 = (s32[]{:T(128)}, f32[32,2048,128]{2,0,1:T(8,128)}, f32[32,256,128]{2,0,1:T(8,128)}, s32[]{:T(128)}, s32[64]{0:T(128)S(1)}, /*index=5*/s32[]{:T(128)}...) while((s32[]{:T(128)}, f32[32,2048,128]{2,0,1:T(8,128)}, ...), condition=%wide.region_3.6_spmd.clone, body=%wide.region_0.5_spmd.clone.sunk | while | flops 1049155 | bytes 10487937 | solution.py:69
  211.6 2.7 broadcast_multiply_fusion.8
  214.3 9.0 scatter_fusion
  223.3 8.0 scatter_fusion.1
  231.3 4.4 copy_bitcast_fusion.5
  235.8 22.6 %copy_bitcast_fusion.1 = f32[32,262144]{1,0:T(8,128)} fusion(f32[32,2048,128]{2,0,1:T(8,128)} %get-tuple-element.609), kind=kLoop, calls=%fused_computation.69 | loop fusion | bytes 67108864 | tf_op jit(solution)/shard_map/reshape | solution.py:86
  258.5 30.0 %reduce-scatter.7.cloned.1.call-done = f32[32,16384]{1,0:T(8,128)} async-done(((f32[32,32768]{1,0:T(8,128)}), f32[32,16384]{1,0:T(8,128)}) %reduce-scatter.7.cloned.1.call-update) | async-done | bytes 2097168 | tf_op jit(solution)/shard_map/reduce_scatter | solution.py:88
  288.4 337.4 %reduce-scatter.5.cloned.1.call-done = f32[32,16384]{1,0:T(8,128)} async-done(((f32[32,262144]{1,0:T(8,128)}), f32[32,16384]{1,0:T(8,128)}) %reduce-scatter.5.cloned.1.call-update) | async-done | bytes 2097168 | tf_op jit(solution)/shard_map/reduce_scatter | solution.py:85
  625.8 2.4 add.216
  629.5 1.8 fusion.52
  631.3 41.0 %all-gather = f32[1024,32]{1,0:T(8,128)S(1)} all-gather(f32[32,32]{1,0:T(8,128)S(1)} %fusion.52), channel_id=2, replica_groups=mesh['row'=2,'col'=16] {'row','col'}, dimensions={0}, use_global_device_ids=true | all-gather | bytes 135168 | tf_op jit(solution)/shard_map/all_gather | solution.py:95
  672.5 58.1 %while.92 = (s32[]{:T(128)}, f32[32,32]{1,0:T(8,128)S(1)}, f32[32,32]{0,1:T(8,128)S(1)}, s32[]{:T(128)}, s32[]{:T(128)}) while((s32[]{:T(128)}, f32[32,32]{1,0:T(8,128)S(1)}, f32[32,32]{0,1:T(8,128)S(1)}, s32[]{:T(128)}, s32[]{:T(128)}) %tuple.192), condition=%wide.region_10.13_spmd.clone.clone, body=%wide.region_7.12_spmd.clone.clone.sunk | while | flops 2401 | bytes 8913 | solution.py:26
  730.6 49.0 %while.93 = (s32[]{:T(128)}, f32[32,32]{1,0:T(8,128)S(1)}, f32[32,32]{1,0:T(8,128)S(1)}, s32[]{:T(128)}, s32[]{:T(128)}) while((s32[]{:T(128)}, f32[32,32]{1,0:T(8,128)S(1)}, f32[32,32]{1,0:T(8,128)S(1)}, s32[]{:T(128)}, s32[]{:T(128)}) %tuple.195), condition=%wide.region_14.17_spmd.clone.clone, body=%wide.region_11.16_spmd.clone.clone.sunk | while | flops 2305 | bytes 6221 | solution.py:43
  779.6 4.4 convolution_convert_fusion
  784.8 28.8 %all-gather.11.cloned.1.call-done = bf16[32,32768]{1,0:T(8,128)(2,1)} async-done(((bf16[32,16384]{1,0:T(8,128)(2,1)}), bf16[32,32768]{1,0:T(8,128)(2,1)}) %all-gather.11.cloned.1.call-update) | async-done | bytes 2097168 | tf_op jit(solution)/shard_map/all_gather | solution.py:80
  813.7 3.3 copy_bitcast_fusion.6
  816.9 2.2 gather_fusion.2
  819.2 2.2 fusion.30
  821.4 121.5 %all-gather.13.cloned.1.call-done = bf16[32,262144]{1,0:T(8,128)(2,1)} async-done(((bf16[32,16384]{1,0:T(8,128)(2,1)}), bf16[32,262144]{1,0:T(8,128)(2,1)}) %all-gather.13.cloned.1.call-update) | async-done | bytes 16777232 | tf_op jit(solution)/shard_map/all_gather | solution.py:81
  942.9 14.5 copy_bitcast_fusion.2
  957.4 6.4 gather_fusion.3
  965.5 11.3 broadcast.314
  976.8 2.6 broadcast.315
  979.3 20.4 %while.91 = (s32[]{:T(128)}, f32[32,2048,128]{2,0,1:T(8,128)}, f32[32,256,128]{2,0,1:T(8,128)}, s32[]{:T(128)}, s32[64]{0:T(128)S(1)}, /*index=5*/s32[]{:T(128)}...) while((s32[]{:T(128)}, f32[32,2048,128]{2,0,1:T(8,128)}, ...), condition=%wide.region_18.21_spmd.clone, body=%wide.region_15.20_spmd.clone.sunk | while | flops 1049155 | bytes 10487937 | solution.py:69
  980.0 2.7 broadcast_multiply_fusion.9
  982.7 9.0 scatter_fusion.2
  991.7 8.0 scatter_fusion.3
  999.7 4.4 copy_bitcast_fusion.4
  1004.2 22.6 %copy_bitcast_fusion = f32[32,262144]{1,0:T(8,128)} fusion(f32[32,2048,128]{2,0,1:T(8,128)} %get-tuple-element.613), kind=kLoop, calls=%fused_computation.68 | loop fusion | bytes 67108864 | tf_op jit(solution)/shard_map/reshape | solution.py:86
  1026.8 30.0 %reduce-scatter.11.cloned.1.call-done = f32[32,16384]{1,0:T(8,128)} async-done(((f32[32,32768]{1,0:T(8,128)}), f32[32,16384]{1,0:T(8,128)}) %reduce-scatter.11.cloned.1.call-update) | async-done | bytes 2097168 | tf_op jit(solution)/shard_map/reduce_scatter | solution.py:88
  1056.8 336.9 %reduce-scatter.9.cloned.1.call-done = f32[32,16384]{1,0:T(8,128)} async-done(((f32[32,262144]{1,0:T(8,128)}), f32[32,16384]{1,0:T(8,128)}) %reduce-scatter.9.cloned.1.call-update) | async-done | bytes 2097168 | tf_op jit(solution)/shard_map/reduce_scatter | solution.py:85
  1393.7 2.4 add.217
  1397.5 1.8 fusion.53
  1399.3 41.0 %all-gather.1 = f32[1024,32]{1,0:T(8,128)S(1)} all-gather(f32[32,32]{1,0:T(8,128)S(1)} %fusion.53), channel_id=3, replica_groups=mesh['row'=2,'col'=16] {'row','col'}, dimensions={0}, use_global_device_ids=true | all-gather | bytes 135168 | tf_op jit(solution)/shard_map/all_gather | solution.py:95
  1440.4 53.9 %while.94 = (s32[]{:T(128)}, f32[32,32]{1,0:T(8,128)S(1)}, f32[32,32]{0,1:T(8,128)S(1)}, s32[]{:T(128)}, s32[]{:T(128)}) while((s32[]{:T(128)}, f32[32,32]{1,0:T(8,128)S(1)}, f32[32,32]{0,1:T(8,128)S(1)}, s32[]{:T(128)}, s32[]{:T(128)}) %tuple.201), condition=%wide.region_25.28_spmd.clone.clone, body=%wide.region_22.27_spmd.clone.clone.sunk | while | flops 2401 | bytes 8913 | solution.py:26
  1494.4 44.3 %while.95 = (s32[]{:T(128)}, f32[32,32]{1,0:T(8,128)S(1)}, f32[32,32]{1,0:T(8,128)S(1)}, s32[]{:T(128)}, s32[]{:T(128)}) while((s32[]{:T(128)}, f32[32,32]{1,0:T(8,128)S(1)}, f32[32,32]{1,0:T(8,128)S(1)}, s32[]{:T(128)}, s32[]{:T(128)}) %tuple.204), condition=%wide.region_29.32_spmd.clone.clone, body=%wide.region_26.31_spmd.clone.clone.sunk | while | flops 2305 | bytes 6221 | solution.py:43
  1538.7 4.8 fusion.54
  (687 shorter events, 164.8 us)
Async XLA Ops:
  6.5 44.4 %copy-start = (bf16[64,128,128]{2,1,0:T(8,128)(2,1)S(1)}, bf16[64,128,128]{2,1,0:T(8,128)(2,1)}, u32[]{:S(2)}) copy-start(bf16[64,128,128]{2,1,0:T(8,128)(2,1)} %param.21) | copy-start | bytes 6291460
  6.5 4.3 copy-start.3
  6.5 4.4 copy-start.4
  6.5 38.8 %all-gather.7.cloned.1.call-start = ((), (), s32[]{:S(2)}) async-start(), calls=%async_computation.4 | async-start | bytes 3145728 | tf_op jit(solution)/shard_map/all_gather | solution.py:80
  9.4 165.1 %all-gather.9.cloned.1.call-start = ((), (), s32[]{:S(2)}) async-start(), calls=%async_computation.5 | async-start | bytes 17825792 | tf_op jit(solution)/shard_map/all_gather | solution.py:81
  10.2 278.3 %reduce-scatter.7.cloned.1.call-start = ((), (), s32[]{:S(2)}) async-start(), calls=%async_computation.7 | async-start | bytes 6291456 | tf_op jit(solution)/shard_map/reduce_scatter | solution.py:88
  235.8 390.0 %reduce-scatter.5.cloned.1.call-start = ((), (), s32[]{:S(2)}) async-start(), calls=%async_computation.6 | async-start | bytes 35651584 | tf_op jit(solution)/shard_map/reduce_scatter | solution.py:85
  258.4 555.2 %all-gather.11.cloned.1.call-start = ((), (), s32[]{:S(2)}) async-start(), calls=%async_computation.8 | async-start | bytes 3145728 | tf_op jit(solution)/shard_map/all_gather | solution.py:80
  628.2 1.3 copy-start.2
  784.0 158.9 %all-gather.13.cloned.1.call-start = ((), (), s32[]{:S(2)}) async-start(), calls=%async_computation.9 | async-start | bytes 17825792 | tf_op jit(solution)/shard_map/all_gather | solution.py:81
  784.6 272.2 %reduce-scatter.11.cloned.1.call-start = ((), (), s32[]{:S(2)}) async-start(), calls=%async_computation.11 | async-start | bytes 6291456 | tf_op jit(solution)/shard_map/reduce_scatter | solution.py:88
  1004.2 389.6 %reduce-scatter.9.cloned.1.call-start = ((), (), s32[]{:S(2)}) async-start(), calls=%async_computation.10 | async-start | bytes 35651584 | tf_op jit(solution)/shard_map/reduce_scatter | solution.py:85
  1396.2 1.4 copy-start.1
Sparse Core Ops, SparseCore 0:
  9.5 35.8 all-gather.6
  47.6 126.9 all-gather.8
  235.9 52.4 reduce-scatter.6
  293.1 332.6 reduce-scatter.4
  784.2 29.4 all-gather.10
  816.0 126.9 all-gather.12
  1004.3 52.4 reduce-scatter.10
  1061.1 332.6 reduce-scatter.8
